TPU v7x, 32 devices: a whole 2x2x4 slice. The times are simulated.
32 devices in a mesh: dp: 16 (over z, y, core), tensor: 2 (over x).
Axes of the slice: x: 2, y: 2, z: 4, core: 2. Of those that a mesh axis runs over, the one named last changes fastest.
Arguments:
- tokens: bfloat16 [32, 448, 1024], P('dp'), may hold values from -6 to 6
- encoded: bfloat16 [32, 1500, 1024], P('dp'), may hold values from -6 to 6
- cotangent: bfloat16 [32, 448, 1024], P('dp'), may hold values from -6 to 6
- self_gain: bfloat16 [1024], replicated, may hold values from 0.5 to 1.5
- self_shift: bfloat16 [1024], replicated, may hold values from -1.75 to 1.75
- self_query: bfloat16 [1024, 1024], P(None, 'tensor'), may hold values from -0.25 to 0.25
- self_query_bias: bfloat16 [1024], P('tensor'), may hold values from -1.75 to 1.75
- self_key: bfloat16 [1024, 1024], P(None, 'tensor'), may hold values from -0.1875 to 0.1875
- self_value: bfloat16 [1024, 1024], P(None, 'tensor'), may hold values from -0.1875 to 0.1875
- self_value_bias: bfloat16 [1024], P('tensor'), may hold values from -1.75 to 1.75
- self_mixer: bfloat16 [1024, 1024], P('tensor'), may hold values from -0.5 to 0.5
- self_mixer_bias: bfloat16 [1024], replicated, may hold values from -1.75 to 1.75
- cross_gain: bfloat16 [1024], replicated, may hold values from 0.5 to 1.5
- cross_shift: bfloat16 [1024], replicated, may hold values from -1.75 to 1.75
- cross_query: bfloat16 [1024, 1024], P(None, 'tensor'), may hold values from -0.25 to 0.25
- cross_query_bias: bfloat16 [1024], P('tensor'), may hold values from -1.75 to 1.75
- cross_key: bfloat16 [1024, 1024], P(None, 'tensor'), may hold values from -0.1875 to 0.1875
- cross_value: bfloat16 [1024, 1024], P(None, 'tensor'), may hold values from -0.1875 to 0.1875
- cross_value_bias: bfloat16 [1024], P('tensor'), may hold values from -1.75 to 1.75
- cross_mixer: bfloat16 [1024, 1024], P('tensor'), may hold values from -0.75 to 0.75
- cross_mixer_bias: bfloat16 [1024], replicated, may hold values from -1.75 to 1.75
- feed_gain: bfloat16 [1024], replicated, may hold values from 0.5 to 1.5
- feed_shift: bfloat16 [1024], replicated, may hold values from -1.75 to 1.75
- expand_weight: bfloat16 [1024, 4096], P(None, 'tensor'), may hold values from -0.1875 to 0.1875
- expand_bias: bfloat16 [4096], P('tensor'), may hold values from -3 to 3
- reduce_weight: bfloat16 [4096, 1024], P('tensor'), may hold values from -0.125 to 0.125
- reduce_bias: bfloat16 [1024], replicated, may hold values from -1.75 to 1.75
Outputs:
- output: float32 [32, 448, 1024], P('dp')
- grad_tokens: float32 [32, 448, 1024], P('dp')
- grad_encoded: float32 [32, 1500, 1024], P('dp', None, 'tensor')
- grad_self_gain: float32 [1024], replicated
- grad_self_shift: float32 [1024], replicated
- grad_self_query: float32 [1024, 1024], P(None, 'tensor')
- grad_self_query_bias: float32 [1024], P('tensor')
- grad_self_key: float32 [1024, 1024], P(None, 'tensor')
- grad_self_value: float32 [1024, 1024], P(None, 'tensor')
- grad_self_value_bias: float32 [1024], P('tensor')
- grad_self_mixer: float32 [1024, 1024], P('tensor')
- grad_self_mixer_bias: float32 [1024], replicated
- grad_cross_gain: float32 [1024], replicated
- grad_cross_shift: float32 [1024], replicated
- grad_cross_query: float32 [1024, 1024], P(None, 'tensor')
- grad_cross_query_bias: float32 [1024], P('tensor')
- grad_cross_key: float32 [1024, 1024], P(None, 'tensor')
- grad_cross_value: float32 [1024, 1024], P(None, 'tensor')
- grad_cross_value_bias: float32 [1024], P('tensor')
- grad_cross_mixer: float32 [1024, 1024], P('tensor')
- grad_cross_mixer_bias: float32 [1024], replicated
- grad_feed_gain: float32 [1024], replicated
- grad_feed_shift: float32 [1024], replicated
- grad_expand_weight: float32 [1024, 4096], P(None, 'tensor')
- grad_expand_bias: float32 [4096], P('tensor')
- grad_reduce_weight: float32 [4096, 1024], P('tensor')
- grad_reduce_bias: float32 [1024], replicated
All inputs are finite; a program needn't handle non-finite values.
Results may differ from a plain program's by a relative error of at most 0.022.
Values may be sent and summed in bfloat16 or wider, within the bound.
No kernel may reach another device: no remote copies, remote signals or barrier semaphores. Data moves between devices by JAX's collectives and lax.ppermute only.
A program may use at most 256 MiB of HBM per device.

v0:
```python
from functools import partial
import math

import jax
import jax.numpy as jnp
from jax import lax
from jax.sharding import PartitionSpec as P

HEAD = 64


EPSILON = 1e-05


def normalize(values, norm_gain, norm_shift):
    row_mean = jnp.mean(values, axis=-1, keepdims=True)
    centered = values - row_mean
    spread = jnp.mean(centered * centered, axis=-1, keepdims=True)
    inverse = lax.rsqrt(spread + EPSILON)
    normed = centered * inverse
    return (normed * norm_gain + norm_shift, normed, inverse)


def normalize_back(grad_out, normed, inverse, norm_gain):
    scaled = grad_out * norm_gain
    centre = jnp.mean(scaled, axis=-1, keepdims=True)
    row_along = jnp.mean(scaled * normed, axis=-1, keepdims=True)
    grad_in = inverse * (scaled - centre - normed * row_along)
    return (grad_in, jnp.sum(grad_out * normed, axis=0), jnp.sum(grad_out, axis=0))


def scores_of(queries, key_heads, causal):
    scaling = 1.0 / math.sqrt(queries.shape[-1])
    scores = (
        jnp.einsum("lhe,khe->hlk", queries, key_heads, preferred_element_type=jnp.float32) * scaling
    )
    if causal:
        row_index = lax.broadcasted_iota(jnp.int32, scores.shape[-2:], 0)
        col_index = lax.broadcasted_iota(jnp.int32, scores.shape[-2:], 1)
        scores = jnp.where(col_index <= row_index, scores, -1e30)
    return scores


def attend(queries, key_heads, value_heads, causal):
    scores = scores_of(queries, key_heads, causal)
    highest = jnp.max(scores, axis=-1, keepdims=True)
    denominator = jnp.sum(jnp.exp(scores - highest), axis=-1, keepdims=True)
    logsum = highest + jnp.log(denominator)
    probs = jnp.exp(scores - logsum)
    mixture = jnp.einsum(
        "hlk,khe->lhe", probs.astype(jnp.bfloat16), value_heads, preferred_element_type=jnp.float32
    )
    return (mixture.astype(jnp.bfloat16), logsum)


def attend_back(grad_mixture, queries, key_heads, value_heads, logsum, causal):
    scaling = 1.0 / math.sqrt(queries.shape[-1])
    probs = jnp.exp(scores_of(queries, key_heads, causal) - logsum)
    grad_probs = jnp.einsum(
        "lhe,khe->hlk", grad_mixture, value_heads, preferred_element_type=jnp.float32
    )
    row_dot = jnp.sum(grad_probs * probs, axis=-1, keepdims=True)
    grad_scores = (probs * (grad_probs - row_dot)).astype(jnp.bfloat16)
    grad_queries = (
        jnp.einsum("hlk,khe->lhe", grad_scores, key_heads, preferred_element_type=jnp.float32)
        * scaling
    ).astype(jnp.bfloat16)
    grad_keys = (
        jnp.einsum("hlk,lhe->khe", grad_scores, queries, preferred_element_type=jnp.float32)
        * scaling
    ).astype(jnp.bfloat16)
    grad_values = jnp.einsum(
        "hlk,lhe->khe", probs.astype(jnp.bfloat16), grad_mixture, preferred_element_type=jnp.float32
    ).astype(jnp.bfloat16)
    return (grad_queries, grad_keys, grad_values)


def project(inputs, weight):
    return jnp.dot(inputs, weight, preferred_element_type=jnp.float32)


def project_back(grads, weight):
    return jnp.einsum("lc,dc->ld", grads, weight, preferred_element_type=jnp.float32)


def weight_grad(inputs, grads):
    return jnp.einsum("ld,lc->dc", inputs, grads, preferred_element_type=jnp.float32)


def column_sum(grads):
    return jnp.sum(grads.astype(jnp.float32), axis=0)


def local(
    tokens,
    encoded,
    cotangent,
    self_gain,
    self_shift,
    self_query,
    self_query_bias,
    self_key,
    self_value,
    self_value_bias,
    self_mixer,
    self_mixer_bias,
    cross_gain,
    cross_shift,
    cross_query,
    cross_query_bias,
    cross_key,
    cross_value,
    cross_value_bias,
    cross_mixer,
    cross_mixer_bias,
    feed_gain,
    feed_shift,
    expand_weight,
    expand_bias,
    reduce_weight,
    reduce_bias,
):
    length = tokens.shape[1]
    frames = encoded.shape[1]
    width = tokens.shape[2]
    local_width = self_query.shape[1]
    head_count = local_width // HEAD
    gain_one = self_gain.astype(jnp.float32)
    gain_two = cross_gain.astype(jnp.float32)
    gain_three = feed_gain.astype(jnp.float32)

    def heads(values, count):
        return values.reshape(count, head_count, HEAD)

    def flat(values, count):
        return values.reshape(count, local_width)

    def micro(totals, inputs):
        clip_tokens, clip_frames, clip_cot = inputs
        source = clip_tokens.astype(jnp.float32)
        first_norm, normed_one, inverse_one = normalize(
            source, gain_one, self_shift.astype(jnp.float32)
        )
        attn_in = first_norm.astype(jnp.bfloat16)
        self_queries = (project(attn_in, self_query) + self_query_bias.astype(jnp.float32)).astype(
            jnp.bfloat16
        )
        self_keys = project(attn_in, self_key).astype(jnp.bfloat16)
        self_values = (project(attn_in, self_value) + self_value_bias.astype(jnp.float32)).astype(
            jnp.bfloat16
        )
        self_heads, self_logsum = attend(
            heads(self_queries, length), heads(self_keys, length), heads(self_values, length), True
        )
        self_mixture = flat(self_heads, length)
        cross_keys = project(clip_frames, cross_key).astype(jnp.bfloat16)
        cross_values = (
            project(clip_frames, cross_value) + cross_value_bias.astype(jnp.float32)
        ).astype(jnp.bfloat16)
        grad_out = clip_cot.astype(jnp.float32)
        self_sum = lax.psum(project(self_mixture, self_mixer), "tensor")
        hidden_one = source + self_sum + self_mixer_bias.astype(jnp.float32)
        second_norm, normed_two, inverse_two = normalize(
            hidden_one, gain_two, cross_shift.astype(jnp.float32)
        )
        cross_in = second_norm.astype(jnp.bfloat16)
        cross_queries = (
            project(cross_in, cross_query) + cross_query_bias.astype(jnp.float32)
        ).astype(jnp.bfloat16)
        cross_heads, cross_logsum = attend(
            heads(cross_queries, length),
            heads(cross_keys, frames),
            heads(cross_values, frames),
            False,
        )
        cross_mixture = flat(cross_heads, length)
        cross_sum = lax.psum(project(cross_mixture, cross_mixer), "tensor")
        hidden_two = hidden_one + cross_sum + cross_mixer_bias.astype(jnp.float32)
        third_norm, normed_three, inverse_three = normalize(
            hidden_two, gain_three, feed_shift.astype(jnp.float32)
        )
        feed_in = third_norm.astype(jnp.bfloat16)
        preact = project(feed_in, expand_weight) + expand_bias.astype(jnp.float32)
        activated = jax.nn.gelu(preact, approximate=False).astype(jnp.bfloat16)
        grad_reduce_bias = jnp.sum(grad_out, axis=0)
        grad_reduce_weight = weight_grad(activated, clip_cot)
        grad_activated = project_back(clip_cot, reduce_weight)
        gelu_value, gelu_pull = jax.vjp(partial(jax.nn.gelu, approximate=False), preact)
        grad_preact = gelu_pull(grad_activated)[0].astype(jnp.bfloat16)
        grad_expand_weight = weight_grad(feed_in, grad_preact)
        grad_expand_bias = column_sum(grad_preact)
        feed_sum = lax.psum(project(activated, reduce_weight), "tensor")
        output = hidden_two + feed_sum + reduce_bias.astype(jnp.float32)
        feed_grad = lax.psum(project_back(grad_preact, expand_weight), "tensor")
        norm_grad, part_feed_gain, part_feed_shift = normalize_back(
            feed_grad, normed_three, inverse_three, gain_three
        )
        grad_two = grad_out + norm_grad
        part_cross_mixer_bias = jnp.sum(grad_two, axis=0)
        two_rounded = grad_two.astype(jnp.bfloat16)
        grad_cross_mixer = weight_grad(cross_mixture, two_rounded)
        grad_cross_mixture = project_back(two_rounded, cross_mixer).astype(jnp.bfloat16)
        cross_query_grad, cross_key_grad, cross_value_grad = attend_back(
            heads(grad_cross_mixture, length),
            heads(cross_queries, length),
            heads(cross_keys, frames),
            heads(cross_values, frames),
            cross_logsum,
            False,
        )
        cross_query_grad = flat(cross_query_grad, length)
        cross_key_grad = flat(cross_key_grad, frames)
        cross_value_grad = flat(cross_value_grad, frames)
        grad_cross_query = weight_grad(cross_in, cross_query_grad)
        grad_cross_query_bias = column_sum(cross_query_grad)
        grad_cross_key = weight_grad(clip_frames, cross_key_grad)
        grad_cross_value = weight_grad(clip_frames, cross_value_grad)
        grad_cross_value_bias = column_sum(cross_value_grad)
        frame_terms = project_back(cross_key_grad, cross_key) + project_back(
            cross_value_grad, cross_value
        )
        grad_encoded = lax.psum_scatter(frame_terms, "tensor", scatter_dimension=1, tiled=True)
        cross_grad = lax.psum(project_back(cross_query_grad, cross_query), "tensor")
        norm_grad, part_cross_gain, part_cross_shift = normalize_back(
            cross_grad, normed_two, inverse_two, gain_two
        )
        grad_one = grad_two + norm_grad
        part_self_mixer_bias = jnp.sum(grad_one, axis=0)
        one_rounded = grad_one.astype(jnp.bfloat16)
        grad_self_mixer = weight_grad(self_mixture, one_rounded)
        grad_self_mixture = project_back(one_rounded, self_mixer).astype(jnp.bfloat16)
        query_grad, key_grad, value_grad = attend_back(
            heads(grad_self_mixture, length),
            heads(self_queries, length),
            heads(self_keys, length),
            heads(self_values, length),
            self_logsum,
            True,
        )
        query_grad = flat(query_grad, length)
        key_grad = flat(key_grad, length)
        value_grad = flat(value_grad, length)
        grad_self_query = weight_grad(attn_in, query_grad)
        grad_self_query_bias = column_sum(query_grad)
        grad_self_key = weight_grad(attn_in, key_grad)
        grad_self_value = weight_grad(attn_in, value_grad)
        grad_self_value_bias = column_sum(value_grad)
        self_terms = (
            project_back(query_grad, self_query)
            + project_back(key_grad, self_key)
            + project_back(value_grad, self_value)
        )
        self_grad = lax.psum(self_terms, "tensor")
        norm_grad, part_self_gain, part_self_shift = normalize_back(
            self_grad, normed_one, inverse_one, gain_one
        )
        grad_tokens = grad_one + norm_grad
        vectors = jnp.stack(
            [
                part_self_gain,
                part_self_shift,
                part_self_mixer_bias,
                part_cross_gain,
                part_cross_shift,
                part_cross_mixer_bias,
                part_feed_gain,
                part_feed_shift,
            ]
        )
        gradients = (
            vectors[0],
            vectors[1],
            grad_self_query,
            grad_self_query_bias,
            grad_self_key,
            grad_self_value,
            grad_self_value_bias,
            grad_self_mixer,
            vectors[2],
            vectors[3],
            vectors[4],
            grad_cross_query,
            grad_cross_query_bias,
            grad_cross_key,
            grad_cross_value,
            grad_cross_value_bias,
            grad_cross_mixer,
            vectors[5],
            vectors[6],
            vectors[7],
            grad_expand_weight,
            grad_expand_bias,
            grad_reduce_weight,
            grad_reduce_bias,
        )
        totals = tuple((left + right for left, right in zip(totals, gradients)))
        return (totals, (output, grad_tokens, grad_encoded))

    shapes = (
        (width,),
        (width,),
        self_query.shape,
        self_query_bias.shape,
        self_key.shape,
        self_value.shape,
        self_value_bias.shape,
        self_mixer.shape,
        (width,),
        (width,),
        (width,),
        cross_query.shape,
        cross_query_bias.shape,
        cross_key.shape,
        cross_value.shape,
        cross_value_bias.shape,
        cross_mixer.shape,
        (width,),
        (width,),
        (width,),
        expand_weight.shape,
        expand_bias.shape,
        reduce_weight.shape,
        (width,),
    )
    start_totals = tuple((jnp.zeros(shape, jnp.float32) for shape in shapes))
    totals, stacked = lax.scan(micro, start_totals, (tokens, encoded, cotangent))
    flat_grads = jnp.concatenate([piece.reshape(-1) for piece in totals])
    devices = lax.axis_size("dp")
    padded = -(-flat_grads.shape[0] // devices) * devices
    flat_grads = jnp.concatenate(
        [flat_grads, jnp.zeros((padded - flat_grads.shape[0],), jnp.float32)]
    )
    share = lax.psum_scatter(flat_grads, "dp", scatter_dimension=0, tiled=True)
    summed = lax.all_gather(share, "dp", axis=0, tiled=True)
    results = []
    offset = 0
    for piece in totals:
        results.append(summed[offset : offset + piece.size].reshape(piece.shape))
        offset = offset + piece.size
    return (
        stacked[0],
        stacked[1],
        stacked[2],
        results[0],
        results[1],
        results[2],
        results[3],
        results[4],
        results[5],
        results[6],
        results[7],
        results[8],
        results[9],
        results[10],
        results[11],
        results[12],
        results[13],
        results[14],
        results[15],
        results[16],
        results[17],
        results[18],
        results[19],
        results[20],
        results[21],
        results[22],
        results[23],
    )


def solution(mesh):
    return jax.shard_map(
        local,
        mesh=mesh,
        in_specs=(
            P("dp", None, None),
            P("dp", None, None),
            P("dp", None, None),
            P(),
            P(),
            P(None, "tensor"),
            P("tensor"),
            P(None, "tensor"),
            P(None, "tensor"),
            P("tensor"),
            P("tensor", None),
            P(),
            P(),
            P(),
            P(None, "tensor"),
            P("tensor"),
            P(None, "tensor"),
            P(None, "tensor"),
            P("tensor"),
            P("tensor", None),
            P(),
            P(),
            P(),
            P(None, "tensor"),
            P("tensor"),
            P("tensor", None),
            P(),
        ),
        out_specs=(
            P("dp", None, None),
            P("dp", None, None),
            P("dp", None, "tensor"),
            P(),
            P(),
            P(None, "tensor"),
            P("tensor"),
            P(None, "tensor"),
            P(None, "tensor"),
            P("tensor"),
            P("tensor", None),
            P(),
            P(),
            P(),
            P(None, "tensor"),
            P("tensor"),
            P(None, "tensor"),
            P(None, "tensor"),
            P("tensor"),
            P("tensor", None),
            P(),
            P(),
            P(),
            P(None, "tensor"),
            P("tensor"),
            P("tensor", None),
            P(),
        ),
        check_vma=False,
    )
```

profile of v0, /device:TPU:0, one launch (start us, length us, event | category | flops | bytes accessed | tf_op | source)
XLA Modules:
  0.0 2641.9 jit_solution(1727320838031355598)
XLA Ops:
  10.4 7.3 copy.101
  17.8 1251.2 %while.63 = (s32[]{:T(128)}, f32[1024]{0:T(1024)}, f32[1024]{0:T(1024)}, f32[1024,512]{1,0:T(8,128)}, f32[512]{0:T(512)}, /*index=5*/f32[1024,512]{1,0:T(8,128)}...) while((s32[]{:T(128)}, f32[1024]{0:T(1024)}, ...), condition=%wide.region_40.41_spmd.clone, body=%wide.region_0.40_spmd.clone.sunk | while | flops 34851655680 | bytes 1151881216 | solution.py:326
  44.5 5.8 fusion.360
  52.0 46.9 %all-reduce.17.cloned.1.call-done = f32[448,1024]{1,0:T(8,128)} async-done(((f32[448,1024]{1,0:T(8,128)}), f32[448,1024]{1,0:T(8,128)}) %all-reduce.17.cloned.1.call-update) | async-done | bytes 1835024 | tf_op jit(solution)/shard_map/while/body/eval_jaxpr/psum | solution.py:161
  110.1 5.7 exponential_reduce_fusion.5
  117.5 10.1 fusion.361
  131.4 56.9 %all-reduce.19.cloned.1.call-done = f32[448,1024]{1,0:T(8,128)} async-done(((f32[448,1024]{1,0:T(8,128)}), f32[448,1024]{1,0:T(8,128)}) %all-reduce.19.cloned.1.call-update) | async-done | bytes 1835024 | tf_op jit(solution)/shard_map/while/body/eval_jaxpr/psum | solution.py:177
  191.6 11.2 multiply_convert_fusion.6
  211.0 57.2 %all-reduce.21.cloned.1.call-done = f32[448,1024]{1,0:T(8,128)} async-done(((f32[448,1024]{1,0:T(8,128)}), f32[448,1024]{1,0:T(8,128)}) %all-reduce.21.cloned.1.call-update) | async-done | bytes 1835024 | tf_op jit(solution)/shard_map/while/body/eval_jaxpr/psum | solution.py:194
  276.3 15.2 multiply_reduce_fusion.23
  291.5 14.7 multiply_convert_fusion.7
  313.7 6.1 fusion.371
  319.8 50.9 %all-reduce.23.cloned.1.call-done = f32[448,1024]{1,0:T(8,128)} async-done(((f32[448,1024]{1,0:T(8,128)}), f32[448,1024]{1,0:T(8,128)}) %all-reduce.23.cloned.1.call-update) | async-done | bytes 1835024 | tf_op jit(solution)/shard_map/while/body/eval_jaxpr/psum | solution.py:223
  379.5 5.2 convert_reduce_fusion.17
  384.7 4.9 multiply_reduce_fusion.25
  402.7 6.1 fusion.373
  410.8 9.8 convert_reduce_fusion.18
  420.6 4.6 convolution_add_fusion.6
  425.9 7.7 select_add_fusion.59
  433.6 6.0 select_add_fusion.57
  469.5 29.6 %all-reduce.25.cloned.1.call-done = (f32[448,1024]{1,0:T(8,128)}, f32[448,1024]{1,0:T(8,128)}) async-done(((f32[448,1024]{1,0:T(8,128)}, f32[448,1024]{1,0:T(8,128)}), (f32[448,1024]{1,0:T(8,128)}, f32[448,1024]{1,0:T(8,128)})) %all-reduce.25.cloned.1.call-update) | async-done | bytes 3670032 | tf_op jit(solution)/shard_map/while/body/eval_jaxpr/psum | solution.py:253
  502.0 4.8 fusion.374
  506.8 70.2 %reduce-scatter.2.cloned.1.call-done = f32[1500,512]{1,0:T(8,128)} async-done(((f32[1500,1024]{1,0:T(8,128)}), f32[1500,512]{1,0:T(8,128)}) %reduce-scatter.2.cloned.1.call-update) | async-done | bytes 3072016 | tf_op jit(solution)/shard_map/while/body/eval_jaxpr/reduce_scatter | solution.py:222
  577.0 8.1 copy.136
  585.3 55.2 %dynamic_update_slice.19 = f32[2,1500,512]{2,0,1:T(2,128)} dynamic-update-slice(f32[2,1500,512]{2,0,1:T(2,128)} %get-tuple-element.1440, f32[1,1500,512]{2,0,1:T(1,128)S(1)} %copy.136, s32[]{:T(128)S(6)} %copy.174, s32[]{:T(128)} %constant.113.clone.1..sunk, s32[]{:T(128)} %constant.113.clone.1..sunk) | dynamic-update-slice | bytes 6144004 | tf_op jit(solution)/shard_map/while/body/jit(dynamic_update_index_in_dim)/dynamic_update_slice | solution.py:326
  667.3 5.7 fusion.360
  674.7 44.5 %all-reduce.17.cloned.1.call-done = f32[448,1024]{1,0:T(8,128)} async-done(((f32[448,1024]{1,0:T(8,128)}), f32[448,1024]{1,0:T(8,128)}) %all-reduce.17.cloned.1.call-update) | async-done | bytes 1835024 | tf_op jit(solution)/shard_map/while/body/eval_jaxpr/psum | solution.py:161
  730.3 5.7 exponential_reduce_fusion.5
  737.6 10.1 fusion.361
  751.3 57.1 %all-reduce.19.cloned.1.call-done = f32[448,1024]{1,0:T(8,128)} async-done(((f32[448,1024]{1,0:T(8,128)}), f32[448,1024]{1,0:T(8,128)}) %all-reduce.19.cloned.1.call-update) | async-done | bytes 1835024 | tf_op jit(solution)/shard_map/while/body/eval_jaxpr/psum | solution.py:177
  811.8 11.2 multiply_convert_fusion.6
  831.4 57.0 %all-reduce.21.cloned.1.call-done = f32[448,1024]{1,0:T(8,128)} async-done(((f32[448,1024]{1,0:T(8,128)}), f32[448,1024]{1,0:T(8,128)}) %all-reduce.21.cloned.1.call-update) | async-done | bytes 1835024 | tf_op jit(solution)/shard_map/while/body/eval_jaxpr/psum | solution.py:194
  896.5 15.2 multiply_reduce_fusion.23
  911.7 14.7 multiply_convert_fusion.7
  933.6 6.1 fusion.371
  939.7 51.1 %all-reduce.23.cloned.1.call-done = f32[448,1024]{1,0:T(8,128)} async-done(((f32[448,1024]{1,0:T(8,128)}), f32[448,1024]{1,0:T(8,128)}) %all-reduce.23.cloned.1.call-update) | async-done | bytes 1835024 | tf_op jit(solution)/shard_map/while/body/eval_jaxpr/psum | solution.py:223
  999.6 5.2 convert_reduce_fusion.17
  1004.9 4.9 multiply_reduce_fusion.25
  1022.9 6.1 fusion.373
  1031.0 10.0 convert_reduce_fusion.18
  1041.0 4.6 convolution_add_fusion.6
  1046.3 10.1 select_add_fusion.59
  1056.5 9.4 select_add_fusion.57
  1066.2 4.5 select_add_fusion.54
  1098.4 20.9 all-reduce.25.cloned.1.call-done
  1122.1 4.8 fusion.374
  1126.9 70.2 %reduce-scatter.2.cloned.1.call-done = f32[1500,512]{1,0:T(8,128)} async-done(((f32[1500,1024]{1,0:T(8,128)}), f32[1500,512]{1,0:T(8,128)}) %reduce-scatter.2.cloned.1.call-update) | async-done | bytes 3072016 | tf_op jit(solution)/shard_map/while/body/eval_jaxpr/reduce_scatter | solution.py:222
  1197.2 8.1 copy.136
  1205.4 55.2 %dynamic_update_slice.19 = f32[2,1500,512]{2,0,1:T(2,128)} dynamic-update-slice(f32[2,1500,512]{2,0,1:T(2,128)} %get-tuple-element.1440, f32[1,1500,512]{2,0,1:T(1,128)S(1)} %copy.136, s32[]{:T(128)S(6)} %copy.174, s32[]{:T(128)} %constant.113.clone.1..sunk, s32[]{:T(128)} %constant.113.clone.1..sunk) | dynamic-update-slice | bytes 6144004 | tf_op jit(solution)/shard_map/while/body/jit(dynamic_update_index_in_dim)/dynamic_update_slice | solution.py:326
  1285.5 5.5 copy.117
  1291.0 5.5 copy.118
  1300.4 19.0 dynamic-update-slice.5
  1319.4 19.0 dynamic-update-slice.6
  1347.4 19.1 dynamic-update-slice.14
  1366.5 18.1 dynamic-update-slice.15
  1390.8 6.7 constant_dynamic-update-slice_fusion.3
  1406.3 563.6 %all-reduce.15.cloned.1.call-done = f32[8401920]{0:T(1024)} async-done(((f32[8401920]{0:T(1024)}), f32[8401920]{0:T(1024)}) %all-reduce.15.cloned.1.call-update) | async-done | bytes 33607696
  1972.1 11.3 broadcast.276
  1983.5 18.0 dynamic-update-slice
  2001.5 566.2 %all-reduce.13.cloned.1.call-done = f32[8401920]{0:T(1024)} async-done(((f32[8401920]{0:T(1024)}), f32[8401920]{0:T(1024)}) %all-reduce.13.cloned.1.call-update) | async-done | bytes 33607696
  2567.8 11.8 fusion.102
  2579.5 9.2 slice.193
  2588.8 11.5 fusion.103
  2620.7 9.2 reshape.431
  (788 shorter events, 325.2 us)
Async XLA Ops:
  18.0 80.9 %all-reduce.17.cloned.1.call-start = ((), (), s32[]{:S(2)}) async-start(), calls=%async_computation.3 | async-start | bytes 3670016 | tf_op jit(solution)/shard_map/while/body/eval_jaxpr/psum | solution.py:161
  18.2 13.9 copy-start.14
  23.7 8.3 copy-start.30
  38.8 149.5 %all-reduce.19.cloned.1.call-start = ((), (), s32[]{:S(2)}) async-start(), calls=%async_computation.4 | async-start | bytes 3670016 | tf_op jit(solution)/shard_map/while/body/eval_jaxpr/psum | solution.py:177
  39.8 61.6 %copy-start.66 = (f32[1024]{0:T(1024)}, f32[1024]{0:T(1024)S(1)}, u32[]{:S(2)}) copy-start(f32[1024]{0:T(1024)S(1)} %convert_element_type.529) | copy-start | bytes 12292 | tf_op jit(solution)/shard_map/while
  44.5 73.0 %copy-start.11 = (bf16[1500,512]{0,1:T(8,128)(2,1)}, bf16[1500,512]{0,1:T(8,128)(2,1)S(1)}, u32[]{:S(2)}) copy-start(bf16[1500,512]{0,1:T(8,128)(2,1)S(1)} %copy.131) | copy-start | bytes 4608004 | tf_op jit(solution)/shard_map/while
  130.9 137.3 %all-reduce.21.cloned.1.call-start = ((), (), s32[]{:S(2)}) async-start(), calls=%async_computation.5 | async-start | bytes 3670016 | tf_op jit(solution)/shard_map/while/body/eval_jaxpr/psum | solution.py:194
  191.6 11.2 copy-start.38
  191.6 11.2 copy-start.133
  210.8 159.9 %all-reduce.23.cloned.1.call-start = ((), (), s32[]{:S(2)}) async-start(), calls=%async_computation.6 | async-start | bytes 3670016 | tf_op jit(solution)/shard_map/while/body/eval_jaxpr/psum | solution.py:223
  313.2 185.9 %all-reduce.25.cloned.1.call-start = ((), (), s32[]{:S(2)}) async-start(), calls=%async_computation.7 | async-start | bytes 7340032 | tf_op jit(solution)/shard_map/while/body/eval_jaxpr/psum | solution.py:253
  379.4 10.2 slice-start
  384.7 13.6 copy-start.45
  401.7 175.3 %reduce-scatter.2.cloned.1.call-start = ((), (), s32[]{:S(2)}) async-start(), calls=%async_computation.8 | async-start | bytes 9240576 | tf_op jit(solution)/shard_map/while/body/eval_jaxpr/reduce_scatter | solution.py:222
  410.8 9.8 copy-start.42
  469.5 32.4 %copy-start.92 = (f32[1024]{0:T(1024)S(1)}, f32[1024]{0:T(1024)}, u32[]{:S(2)}) copy-start(f32[1024]{0:T(1024)} %get-tuple-element.1415) | copy-start | bytes 12292 | tf_op jit(solution)/shard_map/while
  469.5 32.4 %copy-start.95 = (f32[1024]{0:T(1024)S(1)}, f32[1024]{0:T(1024)}, u32[]{:S(2)}) copy-start(f32[1024]{0:T(1024)} %get-tuple-element.1414) | copy-start | bytes 12292 | tf_op jit(solution)/shard_map/while
  585.2 55.3 %copy-start.99 = (bf16[2048]{0:T(1024)(128)(2,1)S(1)}, bf16[2048]{0:T(1024)(128)(2,1)}, u32[]{:S(2)}) copy-start(bf16[2048]{0:T(1024)(128)(2,1)} %get-tuple-element.1620) | copy-start | bytes 12292 | tf_op jit(solution)/shard_map/while
  585.2 55.3 %copy-start.115 = (bf16[1024]{0:T(1024)(128)(2,1)S(1)}, bf16[1024]{0:T(1024)(128)(2,1)}, u32[]{:S(2)}) copy-start(bf16[1024]{0:T(1024)(128)(2,1)} %get-tuple-element.1679) | copy-start | bytes 6148 | tf_op jit(solution)/shard_map/while
  585.2 55.3 %copy-start.117 = (bf16[1024]{0:T(1024)(128)(2,1)S(1)}, bf16[1024]{0:T(1024)(128)(2,1)}, u32[]{:S(2)}) copy-start(bf16[1024]{0:T(1024)(128)(2,1)} %get-tuple-element.1739) | copy-start | bytes 6148 | tf_op jit(solution)/shard_map/while
  585.2 55.2 %copy-start.119 = (bf16[1024]{0:T(1024)(128)(2,1)S(1)}, bf16[1024]{0:T(1024)(128)(2,1)}, u32[]{:S(2)}) copy-start(bf16[1024]{0:T(1024)(128)(2,1)} %get-tuple-element.1800) | copy-start | bytes 6148 | tf_op jit(solution)/shard_map/while
  585.2 55.2 %copy-start.121 = (bf16[1024]{0:T(1024)(128)(2,1)S(1)}, bf16[1024]{0:T(1024)(128)(2,1)}, u32[]{:S(2)}) copy-start(bf16[1024]{0:T(1024)(128)(2,1)} %get-tuple-element.1862) | copy-start | bytes 6148 | tf_op jit(solution)/shard_map/while
  585.2 55.2 %copy-start.123 = (bf16[1024]{0:T(1024)(128)(2,1)S(1)}, bf16[1024]{0:T(1024)(128)(2,1)}, u32[]{:S(2)}) copy-start(bf16[1024]{0:T(1024)(128)(2,1)} %get-tuple-element.1925) | copy-start | bytes 6148 | tf_op jit(solution)/shard_map/while
  585.2 55.2 %copy-start.126 = (bf16[512]{0:T(512)(128)(2,1)S(1)}, bf16[512]{0:T(512)(128)(2,1)}, u32[]{:S(2)}) copy-start(bf16[512]{0:T(512)(128)(2,1)} %get-tuple-element.1989) | copy-start | bytes 3076 | tf_op jit(solution)/shard_map/while
  585.2 55.2 %copy-start.128 = (bf16[512]{0:T(512)(128)(2,1)S(1)}, bf16[512]{0:T(512)(128)(2,1)}, u32[]{:S(2)}) copy-start(bf16[512]{0:T(512)(128)(2,1)} %get-tuple-element.2054) | copy-start | bytes 3076 | tf_op jit(solution)/shard_map/while
  585.3 55.2 %copy-start.130 = (bf16[512]{0:T(512)(128)(2,1)S(1)}, bf16[512]{0:T(512)(128)(2,1)}, u32[]{:S(2)}) copy-start(bf16[512]{0:T(512)(128)(2,1)} %get-tuple-element.2120) | copy-start | bytes 3076 | tf_op jit(solution)/shard_map/while
  640.9 78.2 %all-reduce.17.cloned.1.call-start = ((), (), s32[]{:S(2)}) async-start(), calls=%async_computation.3 | async-start | bytes 3670016 | tf_op jit(solution)/shard_map/while/body/eval_jaxpr/psum | solution.py:161
  641.1 13.8 copy-start.14
  661.7 146.8 %all-reduce.19.cloned.1.call-start = ((), (), s32[]{:S(2)}) async-start(), calls=%async_computation.4 | async-start | bytes 3670016 | tf_op jit(solution)/shard_map/while/body/eval_jaxpr/psum | solution.py:177
  662.6 59.0 %copy-start.66 = (f32[1024]{0:T(1024)}, f32[1024]{0:T(1024)S(1)}, u32[]{:S(2)}) copy-start(f32[1024]{0:T(1024)S(1)} %convert_element_type.529) | copy-start | bytes 12292 | tf_op jit(solution)/shard_map/while
  667.3 70.3 %copy-start.11 = (bf16[1500,512]{0,1:T(8,128)(2,1)}, bf16[1500,512]{0,1:T(8,128)(2,1)S(1)}, u32[]{:S(2)}) copy-start(bf16[1500,512]{0,1:T(8,128)(2,1)S(1)} %copy.131) | copy-start | bytes 4608004 | tf_op jit(solution)/shard_map/while
  751.0 137.3 %all-reduce.21.cloned.1.call-start = ((), (), s32[]{:S(2)}) async-start(), calls=%async_computation.5 | async-start | bytes 3670016 | tf_op jit(solution)/shard_map/while/body/eval_jaxpr/psum | solution.py:194
  811.8 11.2 copy-start.38
  811.8 11.2 copy-start.133
  831.0 159.9 %all-reduce.23.cloned.1.call-start = ((), (), s32[]{:S(2)}) async-start(), calls=%async_computation.6 | async-start | bytes 3670016 | tf_op jit(solution)/shard_map/while/body/eval_jaxpr/psum | solution.py:223
  933.4 185.9 %all-reduce.25.cloned.1.call-start = ((), (), s32[]{:S(2)}) async-start(), calls=%async_computation.7 | async-start | bytes 7340032 | tf_op jit(solution)/shard_map/while/body/eval_jaxpr/psum | solution.py:253
  999.6 10.2 slice-start
  1004.9 13.6 copy-start.45
  1021.9 175.3 %reduce-scatter.2.cloned.1.call-start = ((), (), s32[]{:S(2)}) async-start(), calls=%async_computation.8 | async-start | bytes 9240576 | tf_op jit(solution)/shard_map/while/body/eval_jaxpr/reduce_scatter | solution.py:222
  1030.9 10.0 copy-start.42
  1046.3 10.2 copy-start.69
  1046.3 10.2 copy-start.41
  1056.4 9.6 copy-start.102
  1056.4 9.6 copy-start.105
  1056.4 9.6 copy-start.77
  1056.4 9.6 copy-start.80
  1056.5 9.7 copy-start.71
  1056.5 9.7 copy-start.74
  1098.4 23.7 copy-start.92
  1098.4 23.7 copy-start.95
  1205.3 55.3 %copy-start.99 = (bf16[2048]{0:T(1024)(128)(2,1)S(1)}, bf16[2048]{0:T(1024)(128)(2,1)}, u32[]{:S(2)}) copy-start(bf16[2048]{0:T(1024)(128)(2,1)} %get-tuple-element.1620) | copy-start | bytes 12292 | tf_op jit(solution)/shard_map/while
  1205.3 55.3 %copy-start.115 = (bf16[1024]{0:T(1024)(128)(2,1)S(1)}, bf16[1024]{0:T(1024)(128)(2,1)}, u32[]{:S(2)}) copy-start(bf16[1024]{0:T(1024)(128)(2,1)} %get-tuple-element.1679) | copy-start | bytes 6148 | tf_op jit(solution)/shard_map/while
  1205.3 55.3 %copy-start.117 = (bf16[1024]{0:T(1024)(128)(2,1)S(1)}, bf16[1024]{0:T(1024)(128)(2,1)}, u32[]{:S(2)}) copy-start(bf16[1024]{0:T(1024)(128)(2,1)} %get-tuple-element.1739) | copy-start | bytes 6148 | tf_op jit(solution)/shard_map/while
  1205.4 55.2 %copy-start.119 = (bf16[1024]{0:T(1024)(128)(2,1)S(1)}, bf16[1024]{0:T(1024)(128)(2,1)}, u32[]{:S(2)}) copy-start(bf16[1024]{0:T(1024)(128)(2,1)} %get-tuple-element.1800) | copy-start | bytes 6148 | tf_op jit(solution)/shard_map/while
  1205.4 55.2 %copy-start.121 = (bf16[1024]{0:T(1024)(128)(2,1)S(1)}, bf16[1024]{0:T(1024)(128)(2,1)}, u32[]{:S(2)}) copy-start(bf16[1024]{0:T(1024)(128)(2,1)} %get-tuple-element.1862) | copy-start | bytes 6148 | tf_op jit(solution)/shard_map/while
  1205.4 55.2 %copy-start.123 = (bf16[1024]{0:T(1024)(128)(2,1)S(1)}, bf16[1024]{0:T(1024)(128)(2,1)}, u32[]{:S(2)}) copy-start(bf16[1024]{0:T(1024)(128)(2,1)} %get-tuple-element.1925) | copy-start | bytes 6148 | tf_op jit(solution)/shard_map/while
  1205.4 55.2 %copy-start.126 = (bf16[512]{0:T(512)(128)(2,1)S(1)}, bf16[512]{0:T(512)(128)(2,1)}, u32[]{:S(2)}) copy-start(bf16[512]{0:T(512)(128)(2,1)} %get-tuple-element.1989) | copy-start | bytes 3076 | tf_op jit(solution)/shard_map/while
  1205.4 55.2 %copy-start.128 = (bf16[512]{0:T(512)(128)(2,1)S(1)}, bf16[512]{0:T(512)(128)(2,1)}, u32[]{:S(2)}) copy-start(bf16[512]{0:T(512)(128)(2,1)} %get-tuple-element.2054) | copy-start | bytes 3076 | tf_op jit(solution)/shard_map/while
  1205.4 55.2 %copy-start.130 = (bf16[512]{0:T(512)(128)(2,1)S(1)}, bf16[512]{0:T(512)(128)(2,1)}, u32[]{:S(2)}) copy-start(bf16[512]{0:T(512)(128)(2,1)} %get-tuple-element.2120) | copy-start | bytes 3076 | tf_op jit(solution)/shard_map/while
  1269.0 700.9 %all-reduce.15.cloned.1.call-start = ((), (), s32[]{:S(2)}) async-start(), calls=%async_computation.2 | async-start | bytes 67215360
  1319.4 19.0 copy-start.110
  1366.5 18.1 copy-start.104
  1390.8 8.8 slice-start.7
  1403.8 1164.0 %all-reduce.13.cloned.1.call-start = ((), (), s32[]{:S(2)}) async-start(), calls=%async_computation.1 | async-start | bytes 67215360
  (203 other events, 807.9 us)
Sparse Core Ops, SparseCore 0:
  38.9 59.9 all-reduce.16
  131.0 57.2 all-reduce.18
  210.9 57.2 all-reduce.20
  313.4 57.2 all-reduce.22
  401.8 97.2 all-reduce.24
  501.3 75.7 reduce-scatter.1
  661.8 57.2 all-reduce.16
  751.2 57.2 all-reduce.18
  831.1 57.2 all-reduce.20
  933.5 57.2 all-reduce.22
  1022.0 97.2 all-reduce.24
  1121.4 75.7 reduce-scatter.1
Sparse Core Ops, SparseCore 1:
  1403.9 566.0 all-reduce.14
  2001.6 566.1 all-reduce.12
where the time goes:
time: 2660 us; the launch traced here: 2640 us
  waiting for transfers between devices  1740 us (65%)
  local copies, waits for them, and re-layouts  414 us (16%)
  matrix products  351 us (13%)
  other arithmetic  101 us (4%)
    unnamed x4, waiting for transfers between devices  1130 us
    unnamed x112, local copies, waits for them, and re-layouts  174 us
    reduce_scatter x2, waiting for transfers between devices, micro(): lax.psum_scatter(frame_terms, 'tensor', scatter_dimension=1, tiled=True)  140 us
    dynamic_update_slice x4, local copies, waits for them, and re-layouts, local(): lax.scan(micro, start_totals, (tokens, encoded, cotangent))  127 us
    psum x2, waiting for transfers between devices, micro(): feed_grad = lax.psum(project_back(grad_preact, expand_weight), 'tensor')  114 us
    psum x2, waiting for transfers between devices, micro(): cross_sum = lax.psum(project(cross_mixture, cross_mixer), 'tensor')  114 us
    psum x2, waiting for transfers between devices, micro(): cross_grad = lax.psum(project_back(cross_query_grad, cross_query), 'tensor')  102 us
    psum x2, waiting for transfers between devices, micro(): self_sum = lax.psum(project(self_mixture, self_mixer), 'tensor')  91.4 us
  transfers between devices with their start and end apart: 14, of which 14 were waited for; matrix products, arithmetic and copies ran while one was open for 7% of the time, Pallas kernels for 0%

commit v1 on v0

v1 whole, which is shorter than its diff:
```python
import math

import jax
import jax.numpy as jnp
from jax import lax
from jax.sharding import PartitionSpec as P

HEAD = 64
EPSILON = 1e-05
F32 = jnp.float32
BF16 = jnp.bfloat16


def normalize(values, norm_gain, norm_shift):
    row_mean = jnp.mean(values, axis=-1, keepdims=True)
    centered = values - row_mean
    spread = jnp.mean(centered * centered, axis=-1, keepdims=True)
    inverse = lax.rsqrt(spread + EPSILON)
    normed = centered * inverse
    return (normed * norm_gain + norm_shift, normed, inverse)


def normalize_back(grad_out, normed, inverse, norm_gain):
    scaled = grad_out * norm_gain
    centre = jnp.mean(scaled, axis=-1, keepdims=True)
    row_along = jnp.mean(scaled * normed, axis=-1, keepdims=True)
    grad_in = inverse * (scaled - centre - normed * row_along)
    return (grad_in, jnp.sum(grad_out * normed, axis=0), jnp.sum(grad_out, axis=0))


def scores_of(queries, key_heads, causal):
    scaling = 1.0 / math.sqrt(queries.shape[-1])
    scores = jnp.einsum("lhe,khe->hlk", queries, key_heads, preferred_element_type=F32) * scaling
    if causal:
        row_index = lax.broadcasted_iota(jnp.int32, scores.shape[-2:], 0)
        col_index = lax.broadcasted_iota(jnp.int32, scores.shape[-2:], 1)
        scores = jnp.where(col_index <= row_index, scores, -1e30)
    return scores


def attend(queries, key_heads, value_heads, causal):
    scores = scores_of(queries, key_heads, causal)
    highest = jnp.max(scores, axis=-1, keepdims=True)
    denominator = jnp.sum(jnp.exp(scores - highest), axis=-1, keepdims=True)
    logsum = highest + jnp.log(denominator)
    probs = jnp.exp(scores - logsum)
    mixture = jnp.einsum(
        "hlk,khe->lhe", probs.astype(BF16), value_heads, preferred_element_type=F32
    )
    return (mixture.astype(BF16), logsum)


def attend_back(grad_mixture, queries, key_heads, value_heads, logsum, causal):
    scaling = 1.0 / math.sqrt(queries.shape[-1])
    probs = jnp.exp(scores_of(queries, key_heads, causal) - logsum)
    grad_probs = jnp.einsum("lhe,khe->hlk", grad_mixture, value_heads, preferred_element_type=F32)
    row_dot = jnp.sum(grad_probs * probs, axis=-1, keepdims=True)
    grad_scores = (probs * (grad_probs - row_dot)).astype(BF16)
    grad_queries = (
        jnp.einsum("hlk,khe->lhe", grad_scores, key_heads, preferred_element_type=F32) * scaling
    ).astype(BF16)
    grad_keys = (
        jnp.einsum("hlk,lhe->khe", grad_scores, queries, preferred_element_type=F32) * scaling
    ).astype(BF16)
    grad_values = jnp.einsum(
        "hlk,lhe->khe", probs.astype(BF16), grad_mixture, preferred_element_type=F32
    ).astype(BF16)
    return (grad_queries, grad_keys, grad_values)


def project(inputs, weight):
    return jnp.dot(inputs, weight, preferred_element_type=F32)


def project_back(grads, weight):
    return jnp.einsum("lc,dc->ld", grads, weight, preferred_element_type=F32)


def weight_grad(inputs, grads):
    left = jnp.concatenate(inputs, axis=0)
    right = jnp.concatenate(grads, axis=0)
    return jnp.einsum("ld,lc->dc", left, right, preferred_element_type=F32).astype(BF16)


def column_sum(grads):
    return jnp.sum(grads.astype(F32), axis=0)


def tensor_sum(partial):
    if lax.axis_size("tensor") != 2:
        return lax.psum(partial, "tensor")
    mine = lax.optimization_barrier(partial.astype(BF16))
    other = lax.ppermute(mine, "tensor", [(0, 1), (1, 0)])
    return mine.astype(F32) + other.astype(F32)


def dp_sum(grads):
    share = lax.psum_scatter(grads, "dp", scatter_dimension=0, tiled=True)
    return lax.all_gather(share, "dp", axis=0, tiled=True)


def local(
    tokens,
    encoded,
    cotangent,
    self_gain,
    self_shift,
    self_query,
    self_query_bias,
    self_key,
    self_value,
    self_value_bias,
    self_mixer,
    self_mixer_bias,
    cross_gain,
    cross_shift,
    cross_query,
    cross_query_bias,
    cross_key,
    cross_value,
    cross_value_bias,
    cross_mixer,
    cross_mixer_bias,
    feed_gain,
    feed_shift,
    expand_weight,
    expand_bias,
    reduce_weight,
    reduce_bias,
):
    clips, length, width = tokens.shape
    frames = encoded.shape[1]
    local_width = self_query.shape[1]
    head_count = local_width // HEAD
    gain_one = self_gain.astype(F32)
    gain_two = cross_gain.astype(F32)
    gain_three = feed_gain.astype(F32)
    each = range(clips)

    def heads(values):
        return values.reshape(values.shape[0], head_count, HEAD)

    def flat(values):
        return values.reshape(values.shape[0], local_width)

    source, normed_one, inverse_one, attn_in = [], [], [], []
    self_queries, self_keys, self_values = [], [], []
    self_mixture, self_logsum, self_sum = [], [], []
    cross_keys, cross_values = [], []
    for i in each:
        source.append(tokens[i].astype(F32))
        normed, plain, inverse = normalize(source[i], gain_one, self_shift.astype(F32))
        normed_one.append(plain)
        inverse_one.append(inverse)
        attn_in.append(normed.astype(BF16))
        self_queries.append(
            (project(attn_in[i], self_query) + self_query_bias.astype(F32)).astype(BF16)
        )
        self_keys.append(project(attn_in[i], self_key).astype(BF16))
        self_values.append(
            (project(attn_in[i], self_value) + self_value_bias.astype(F32)).astype(BF16)
        )
        mixed, logsum = attend(heads(self_queries[i]), heads(self_keys[i]), heads(self_values[i]), True)
        self_mixture.append(flat(mixed))
        self_logsum.append(logsum)
        self_sum.append(tensor_sum(project(self_mixture[i], self_mixer)))
    for i in each:
        cross_keys.append(project(encoded[i], cross_key).astype(BF16))
        cross_values.append(
            (project(encoded[i], cross_value) + cross_value_bias.astype(F32)).astype(BF16)
        )

    hidden_one, normed_two, inverse_two, cross_in = [], [], [], []
    cross_queries, cross_mixture, cross_logsum, cross_sum = [], [], [], []
    for i in each:
        hidden_one.append(source[i] + self_sum[i] + self_mixer_bias.astype(F32))
        normed, plain, inverse = normalize(hidden_one[i], gain_two, cross_shift.astype(F32))
        normed_two.append(plain)
        inverse_two.append(inverse)
        cross_in.append(normed.astype(BF16))
        cross_queries.append(
            (project(cross_in[i], cross_query) + cross_query_bias.astype(F32)).astype(BF16)
        )
        mixed, logsum = attend(
            heads(cross_queries[i]), heads(cross_keys[i]), heads(cross_values[i]), False
        )
        cross_mixture.append(flat(mixed))
        cross_logsum.append(logsum)
        cross_sum.append(tensor_sum(project(cross_mixture[i], cross_mixer)))

    hidden_two, normed_three, inverse_three, feed_in = [], [], [], []
    activated, grad_preact, feed_grad, feed_sum = [], [], [], []
    for i in each:
        hidden_two.append(hidden_one[i] + cross_sum[i] + cross_mixer_bias.astype(F32))
        normed, plain, inverse = normalize(hidden_two[i], gain_three, feed_shift.astype(F32))
        normed_three.append(plain)
        inverse_three.append(inverse)
        feed_in.append(normed.astype(BF16))
        preact = project(feed_in[i], expand_weight) + expand_bias.astype(F32)
        grad_activated = project_back(cotangent[i], reduce_weight)
        cdf = 0.5 * (1.0 + lax.erf(preact * (1.0 / math.sqrt(2.0))))
        density = jnp.exp(-0.5 * preact * preact) * (1.0 / math.sqrt(2.0 * math.pi))
        activated.append((preact * cdf).astype(BF16))
        grad_preact.append((grad_activated * (cdf + preact * density)).astype(BF16))
        feed_grad.append(tensor_sum(project_back(grad_preact[i], expand_weight)))
    for i in each:
        feed_sum.append(tensor_sum(project(activated[i], reduce_weight)))
    output = [hidden_two[i] + feed_sum[i] + reduce_bias.astype(F32) for i in each]
    grad_out = [cotangent[i].astype(F32) for i in each]
    grad_reduce_weight = dp_sum(weight_grad(activated, [cotangent[i] for i in each]))
    grad_expand_weight = dp_sum(weight_grad(feed_in, grad_preact))
    grad_reduce_bias = sum(jnp.sum(grad_out[i], axis=0) for i in each)
    grad_expand_bias = sum(column_sum(grad_preact[i]) for i in each)

    grad_two, two_rounded, feed_gains, feed_shifts = [], [], [], []
    cross_query_grad, cross_key_grad, cross_value_grad = [], [], []
    cross_grad = []
    for i in each:
        norm_grad, part_gain, part_shift = normalize_back(
            feed_grad[i], normed_three[i], inverse_three[i], gain_three
        )
        feed_gains.append(part_gain)
        feed_shifts.append(part_shift)
        grad_two.append(grad_out[i] + norm_grad)
        two_rounded.append(grad_two[i].astype(BF16))
        grad_cross_mixture = project_back(two_rounded[i], cross_mixer).astype(BF16)
        query_grad, key_grad, value_grad = attend_back(
            heads(grad_cross_mixture),
            heads(cross_queries[i]),
            heads(cross_keys[i]),
            heads(cross_values[i]),
            cross_logsum[i],
            False,
        )
        cross_query_grad.append(flat(query_grad))
        cross_key_grad.append(flat(key_grad))
        cross_value_grad.append(flat(value_grad))
        cross_grad.append(tensor_sum(project_back(cross_query_grad[i], cross_query)))
    grad_cross_mixer = dp_sum(weight_grad(cross_mixture, two_rounded))
    grad_cross_query = dp_sum(weight_grad(cross_in, cross_query_grad))
    frames_in = [encoded[i] for i in each]
    grad_cross_key = dp_sum(weight_grad(frames_in, cross_key_grad))
    grad_cross_value = dp_sum(weight_grad(frames_in, cross_value_grad))
    part_cross_mixer_bias = sum(jnp.sum(grad_two[i], axis=0) for i in each)
    grad_cross_query_bias = sum(column_sum(cross_query_grad[i]) for i in each)
    grad_cross_value_bias = sum(column_sum(cross_value_grad[i]) for i in each)

    grad_one, one_rounded, cross_gains, cross_shifts = [], [], [], []
    query_grads, key_grads, value_grads, self_grad = [], [], [], []
    for i in each:
        norm_grad, part_gain, part_shift = normalize_back(
            cross_grad[i], normed_two[i], inverse_two[i], gain_two
        )
        cross_gains.append(part_gain)
        cross_shifts.append(part_shift)
        grad_one.append(grad_two[i] + norm_grad)
        one_rounded.append(grad_one[i].astype(BF16))
        grad_self_mixture = project_back(one_rounded[i], self_mixer).astype(BF16)
        query_grad, key_grad, value_grad = attend_back(
            heads(grad_self_mixture),
            heads(self_queries[i]),
            heads(self_keys[i]),
            heads(self_values[i]),
            self_logsum[i],
            True,
        )
        query_grads.append(flat(query_grad))
        key_grads.append(flat(key_grad))
        value_grads.append(flat(value_grad))
        self_terms = (
            project_back(query_grads[i], self_query)
            + project_back(key_grads[i], self_key)
            + project_back(value_grads[i], self_value)
        )
        self_grad.append(tensor_sum(self_terms))
    grad_self_mixer = dp_sum(weight_grad(self_mixture, one_rounded))
    grad_self_query = dp_sum(weight_grad(attn_in, query_grads))
    grad_self_key = dp_sum(weight_grad(attn_in, key_grads))
    grad_self_value = dp_sum(weight_grad(attn_in, value_grads))
    part_self_mixer_bias = sum(jnp.sum(grad_one[i], axis=0) for i in each)
    grad_self_query_bias = sum(column_sum(query_grads[i]) for i in each)
    grad_self_value_bias = sum(column_sum(value_grads[i]) for i in each)

    grad_encoded = []
    members = lax.axis_size("tensor")
    share = width // members
    for i in each:
        if members == 2:
            me = lax.axis_index("tensor")

            def terms(part):
                rows_key = lax.dynamic_slice_in_dim(cross_key, part * share, share, 0)
                rows_value = lax.dynamic_slice_in_dim(cross_value, part * share, share, 0)
                return project_back(cross_key_grad[i], rows_key) + project_back(
                    cross_value_grad[i], rows_value
                )

            other = lax.ppermute(terms(1 - me).astype(BF16), "tensor", [(0, 1), (1, 0)])
            grad_encoded.append(terms(me) + other.astype(F32))
        else:
            frame_terms = project_back(cross_key_grad[i], cross_key) + project_back(
                cross_value_grad[i], cross_value
            )
            grad_encoded.append(
                lax.psum_scatter(frame_terms, "tensor", scatter_dimension=1, tiled=True)
            )

    self_gains, self_shifts, grad_tokens = [], [], []
    for i in each:
        norm_grad, part_gain, part_shift = normalize_back(
            self_grad[i], normed_one[i], inverse_one[i], gain_one
        )
        self_gains.append(part_gain)
        self_shifts.append(part_shift)
        grad_tokens.append(grad_one[i] + norm_grad)

    vectors = [
        sum(self_gains),
        sum(self_shifts),
        part_self_mixer_bias,
        sum(cross_gains),
        sum(cross_shifts),
        part_cross_mixer_bias,
        sum(feed_gains),
        sum(feed_shifts),
        grad_reduce_bias,
        grad_self_query_bias,
        grad_self_value_bias,
        grad_cross_query_bias,
        grad_cross_value_bias,
        grad_expand_bias,
    ]
    summed = lax.psum(jnp.concatenate(vectors), "dp")
    pieces, offset = [], 0
    for piece in vectors:
        pieces.append(summed[offset : offset + piece.size])
        offset = offset + piece.size
    return (
        jnp.stack(output),
        jnp.stack(grad_tokens),
        jnp.stack(grad_encoded),
        pieces[0],
        pieces[1],
        grad_self_query.astype(F32),
        pieces[9],
        grad_self_key.astype(F32),
        grad_self_value.astype(F32),
        pieces[10],
        grad_self_mixer.astype(F32),
        pieces[2],
        pieces[3],
        pieces[4],
        grad_cross_query.astype(F32),
        pieces[11],
        grad_cross_key.astype(F32),
        grad_cross_value.astype(F32),
        pieces[12],
        grad_cross_mixer.astype(F32),
        pieces[5],
        pieces[6],
        pieces[7],
        grad_expand_weight.astype(F32),
        pieces[13],
        grad_reduce_weight.astype(F32),
        pieces[8],
    )


def solution(mesh):
    rows = P("dp", None, None)
    column, row, part = P(None, "tensor"), P("tensor", None), P("tensor")
    return jax.shard_map(
        local,
        mesh=mesh,
        in_specs=(
            rows,
            rows,
            rows,
            P(),
            P(),
            column,
            part,
            column,
            column,
            part,
            row,
            P(),
            P(),
            P(),
            column,
            part,
            column,
            column,
            part,
            row,
            P(),
            P(),
            P(),
            column,
            part,
            row,
            P(),
        ),
        out_specs=(
            rows,
            rows,
            P("dp", None, "tensor"),
            P(),
            P(),
            column,
            part,
            column,
            column,
            part,
            row,
            P(),
            P(),
            P(),
            column,
            part,
            column,
            column,
            part,
            row,
            P(),
            P(),
            P(),
            column,
            part,
            row,
            P(),
        ),
        check_vma=False,
    )
```

time: 2660 us -> 1480 us (0.56)
  waiting for transfers between devices: 1740 us -> 843 us
  local copies, waits for them, and re-layouts: 414 us -> 105 us
  blocking collectives: 0 us -> 58 us
  matrix products: 351 us -> 295 us
  other arithmetic: 101 us -> 140 us
    unnamed x4 -> x20, waiting for transfers between devices: 1130 us -> 1.45 us
    psum x10 -> x0, waiting for transfers between devices: 472 us -> none  [the longest x2 114 us: micro(): feed_grad = lax.psum(project_back(grad_preact, expand_weight), 'tensor')]
    reduce_scatter x2 -> x10, waiting for transfers between devices: 140 us -> 430 us  [dp_sum(): share = lax.psum_scatter(grads, 'dp', scatter_dimension=0, tiled=True)]
    all_gather x0 -> x10, waiting for transfers between devices: none -> 255 us  [dp_sum(): return lax.all_gather(share, 'dp', axis=0, tiled=True)]
    ppermute x0 -> x14, waiting for transfers between devices: none -> 157 us  [the longest x12 103 us: tensor_sum(): other = lax.ppermute(mine, 'tensor', [(0, 1), (1, 0)])]
    dynamic_update_slice x4 -> x0, local copies, waits for them, and re-layouts: 127 us -> none  [local(): lax.scan(micro, start_totals, (tokens, encoded, cotangent))]
    unnamed x112 -> x353, local copies, waits for them, and re-layouts: 174 us -> 51.9 us
    dot_general x76 -> x70, matrix products: 302 us -> 234 us  [the longest x24 53.9 us: project_back(): return jnp.einsum('lc,dc->ld', grads, weight, preferred_element_type=F32)]
  transfers between devices with their start and end apart: 14 -> 34, of which waited for: 14 -> 26; matrix products, arithmetic and copies ran while one was open for 7% -> 20% of each run, Pallas kernels for 0% -> 0%
where the time goes in v1:
time: 1480 us
  waiting for transfers between devices  843 us (57%)
  matrix products  295 us (20%)
  other arithmetic  140 us (9%)
  local copies, waits for them, and re-layouts  105 us (7%)
  blocking collectives  58 us (4%)
  starting transfers between devices  17.6 us (1%)
  between operations  16.8 us (1%)
    reduce_scatter x10, waiting for transfers between devices, dp_sum(): share = lax.psum_scatter(grads, 'dp', scatter_dimension=0, tiled=True)  430 us
    all_gather x10, waiting for transfers between devices, dp_sum(): return lax.all_gather(share, 'dp', axis=0, tiled=True)  255 us
    ppermute x12, waiting for transfers between devices, tensor_sum(): other = lax.ppermute(mine, 'tensor', [(0, 1), (1, 0)])  103 us
    psum x1, blocking collectives, local(): summed = lax.psum(jnp.concatenate(vectors), 'dp')  58 us
    ppermute x2, waiting for transfers between devices, local(): other = lax.ppermute(terms(1 - me).astype(BF16), 'tensor', [(0, 1), (1, 0)])  54 us
    dot_general x24, matrix products, project_back(): return jnp.einsum('lc,dc->ld', grads, weight, preferred_element_type=F32)  53.9 us
    unnamed x353, local copies, waits for them, and re-layouts  51.9 us
    dot_general x20, matrix products, project(): return jnp.dot(inputs, weight, preferred_element_type=F32)  51.5 us
  transfers between devices with their start and end apart: 34, of which 26 were waited for; matrix products, arithmetic and copies ran while one was open for 20% of the time, Pallas kernels for 0%

profile of v1, /device:TPU:0, one launch (start us, length us, event | category | flops | bytes accessed | tf_op | source)
XLA Modules:
  0.0 1476.1 jit_solution(17825031323830864179)
XLA Ops:
  41.3 10.0 fusion.219
  51.3 8.1 copy_bitcast_fusion
  59.4 4.8 fusion.34
  66.7 4.8 convolution_convert_fusion.3
  81.7 4.7 multiply_reduce_fusion.3
  86.4 5.9 exponential_reduce_fusion.1
  93.8 12.3 fusion.135
  108.5 21.7 %collective-permute-done.1 = bf16[448,1024]{1,0:T(8,128)(2,1)S(1)} collective-permute-done((bf16[448,1024]{1,0:T(8,128)(2,1)S(1)}, bf16[448,1024]{1,0:T(8,128)(2,1)S(1)}, u32[]{:S(2)}, u32[]{:S(2)}) %collective-permute-start.1) | collective-permute-done | bytes 917536 | tf_op jit(solution)/shard_map/ppermute | solution.py:93
  152.1 15.1 %collective-permute-done.6 = bf16[448,1024]{1,0:T(8,128)(2,1)} collective-permute-done((bf16[448,1024]{1,0:T(8,128)(2,1)}, bf16[448,1024]{1,0:T(8,128)(2,1)}, u32[]{:S(2)}, u32[]{:S(2)}) %collective-permute-start.6) | collective-permute-done | bytes 917536 | tf_op jit(solution)/shard_map/ppermute | solution.py:93
  170.8 13.8 collective-permute-done.2
  184.5 4.5 convert_reduce_fusion.4
  194.8 15.2 %multiply_reduce_fusion.1 = (f32[8,448]{1,0:T(8,128)S(1)}, f32[8,448,1500]{2,1,0:T(8,128)}) fusion(f32[8,448,1500]{2,1,0:T(8,128)} %copy-done.1, f32[8,448]{1,0:T(8,128)S(1)} %log_add_fusion.2, bf16[448,8,64]{0,2,1:T(8,128)(2,1)} %bitcast.336, bf16[1500,8,64]{0,2,1:T(8,128)(2,1)} %bitcast.325), kind=kOutput, calls=%fused_computation.3 | convolution fusion | flops 709628416 | bytes 45031424 | tf_op jit(solution)/shard_map/lhe,khe->hlk/dot_general | solution.py:56
  210.0 15.2 %multiply_convert_fusion.1 = bf16[8,448,1500]{2,1,0:T(8,128)(2,1)S(1)} fusion(f32[8,448,1500]{2,1,0:T(8,128)} %get-tuple-element.165, f32[8,448,1500]{2,1,0:T(8,128)} %copy-done.1, f32[8,448]{1,0:T(8,128)S(1)} %get-tuple-element.164, f32[8,448]{1,0:T(8,128)S(1)} %log_add_fusion.2), kind=kLoop, calls=%fused_computation.2 | loop fusion | flops 26880000 | bytes 53788672 | tf_op jit(solution)/shard_map/convert_element_type | solution.py:58
  225.3 4.8 convert_reduce_fusion.9
  242.4 5.5 fusion.222
  247.9 5.9 collective-permute-done.7
  265.5 9.1 multiply_reduce_fusion.5
  275.2 5.2 multiply_convert_fusion.3
  291.6 5.0 fusion.35
  299.4 5.4 collective-permute-done.3
  312.4 4.2 multiply_reduce_fusion.2
  316.6 5.7 exponential_reduce_fusion
  324.4 10.1 fusion.138
  337.9 10.9 convert_reduce_fusion.3
  348.8 6.3 collective-permute-done.4
  360.9 4.0 convert_reduce_fusion
  374.5 15.8 %collective-permute-done.9 = bf16[448,1024]{1,0:T(8,128)(2,1)S(1)} collective-permute-done((bf16[448,1024]{1,0:T(8,128)(2,1)S(1)}, bf16[448,1024]{1,0:T(8,128)(2,1)S(1)}, u32[]{:S(2)}, u32[]{:S(2)}) %collective-permute-start.9) | collective-permute-done | bytes 917536 | tf_op jit(solution)/shard_map/ppermute | solution.py:93
  391.9 12.4 collective-permute-done.5
  416.9 11.9 convert_reduce_fusion.2
  430.0 5.4 fusion.113
  435.5 15.4 %multiply_reduce_fusion = (f32[8,448]{1,0:T(8,128)S(1)}, f32[8,448,1500]{2,1,0:T(8,128)}) fusion(f32[8,448,1500]{2,1,0:T(8,128)} %copy-done.2, f32[8,448]{1,0:T(8,128)S(1)} %log_add_fusion, bf16[448,8,64]{0,2,1:T(8,128)(2,1)} %bitcast.339, bf16[1500,8,64]{0,2,1:T(8,128)(2,1)} %bitcast.322), kind=kOutput, calls=%fused_computation.1 | convolution fusion | flops 709628416 | bytes 45031424 | tf_op jit(solution)/shard_map/lhe,khe->hlk/dot_general | solution.py:56
  451.2 14.9 %multiply_convert_fusion = bf16[8,448,1500]{2,1,0:T(8,128)(2,1)S(1)} fusion(f32[8,448,1500]{2,1,0:T(8,128)} %get-tuple-element.172, f32[8,448,1500]{2,1,0:T(8,128)} %copy-done.2, f32[8,448]{1,0:T(8,128)S(1)} %get-tuple-element.171, f32[8,448]{1,0:T(8,128)S(1)} %log_add_fusion), kind=kLoop, calls=%fused_computation | loop fusion | flops 26880000 | bytes 53788672 | tf_op jit(solution)/shard_map/convert_element_type | solution.py:58
  474.0 5.4 fusion.110
  479.5 8.1 convert_reduce_fusion.8
  491.0 5.9 convert_reduce_fusion.11
  499.9 6.4 collective-permute-done.10
  514.3 5.3 convert_reduce_fusion.10
  528.4 4.7 multiply_reduce_fusion.4
  533.1 4.2 multiply_convert_fusion.2
  552.6 6.2 convolution_convert_fusion
  560.3 8.2 convolution_convert_fusion.1
  569.8 23.5 %reduce-scatter.21.cloned.1.call-done = bf16[64,512]{1,0:T(8,128)(2,1)} async-done(((bf16[1024,512]{1,0:T(8,128)(2,1)}), bf16[64,512]{1,0:T(8,128)(2,1)}) %reduce-scatter.21.cloned.1.call-update) | async-done | bytes 65552 | tf_op jit(solution)/shard_map/reduce_scatter | solution.py:98
  593.4 60.1 %reduce-scatter.19.cloned.1.call-done = bf16[64,512]{1,0:T(8,128)(2,1)} async-done(((bf16[1024,512]{1,0:T(8,128)(2,1)}), bf16[64,512]{1,0:T(8,128)(2,1)}) %reduce-scatter.19.cloned.1.call-update) | async-done | bytes 65552 | tf_op jit(solution)/shard_map/reduce_scatter | solution.py:98
  653.5 60.1 %reduce-scatter.15.cloned.1.call-done = bf16[64,512]{1,0:T(8,128)(2,1)} async-done(((bf16[1024,512]{1,0:T(8,128)(2,1)}), bf16[64,512]{1,0:T(8,128)(2,1)}) %reduce-scatter.15.cloned.1.call-update) | async-done | bytes 65552 | tf_op jit(solution)/shard_map/reduce_scatter | solution.py:98
  713.7 60.2 %reduce-scatter.17.cloned.1.call-done = bf16[32,1024]{1,0:T(8,128)(2,1)} async-done(((bf16[512,1024]{1,0:T(8,128)(2,1)}), bf16[32,1024]{1,0:T(8,128)(2,1)}) %reduce-scatter.17.cloned.1.call-update) | async-done | bytes 65552 | tf_op jit(solution)/shard_map/reduce_scatter | solution.py:98
  773.9 60.8 %reduce-scatter.11.cloned.1.call-done = bf16[64,512]{1,0:T(8,128)(2,1)} async-done(((bf16[1024,512]{1,0:T(8,128)(2,1)}), bf16[64,512]{1,0:T(8,128)(2,1)}) %reduce-scatter.11.cloned.1.call-update) | async-done | bytes 65552 | tf_op jit(solution)/shard_map/reduce_scatter | solution.py:98
  834.8 60.8 %reduce-scatter.13.cloned.1.call-done = bf16[64,512]{1,0:T(8,128)(2,1)} async-done(((bf16[1024,512]{1,0:T(8,128)(2,1)}), bf16[64,512]{1,0:T(8,128)(2,1)}) %reduce-scatter.13.cloned.1.call-update) | async-done | bytes 65552 | tf_op jit(solution)/shard_map/reduce_scatter | solution.py:98
  895.7 76.3 %reduce-scatter.29.cloned.1.call-done = bf16[128,1024]{1,0:T(8,128)(2,1)} async-done(((bf16[2048,1024]{1,0:T(8,128)(2,1)}), bf16[128,1024]{1,0:T(8,128)(2,1)}) %reduce-scatter.29.cloned.1.call-update) | async-done | bytes 262160 | tf_op jit(solution)/shard_map/reduce_scatter | solution.py:98
  984.0 29.0 %collective-permute-done.12 = bf16[1500,512]{1,0:T(8,128)(2,1)} collective-permute-done((bf16[1500,512]{1,0:T(8,128)(2,1)}, bf16[1500,512]{1,0:T(8,128)(2,1)}, u32[]{:S(2)}, u32[]{:S(2)}) %collective-permute-start.12) | collective-permute-done | bytes 1536032 | tf_op jit(solution)/shard_map/ppermute | solution.py:298
  1013.0 4.1 add_bitcast_fusion.1
  1019.8 28.3 %reduce-scatter.27.cloned.1.call-done = bf16[64,2048]{1,0:T(8,128)(2,1)} async-done(((bf16[1024,2048]{1,0:T(8,128)(2,1)}), bf16[64,2048]{1,0:T(8,128)(2,1)}) %reduce-scatter.27.cloned.1.call-update) | async-done | bytes 262160 | tf_op jit(solution)/shard_map/reduce_scatter | solution.py:98
  1048.1 4.7 fusion.37
  1064.7 25.0 %collective-permute-done.13 = bf16[1500,512]{1,0:T(8,128)(2,1)} collective-permute-done((bf16[1500,512]{1,0:T(8,128)(2,1)}, bf16[1500,512]{1,0:T(8,128)(2,1)}, u32[]{:S(2)}, u32[]{:S(2)}) %collective-permute-start.13) | collective-permute-done | bytes 1536032 | tf_op jit(solution)/shard_map/ppermute | solution.py:298
  1094.6 12.7 copy.122
  1111.8 58.0 %psum.7 = f32[13312]{0:T(1024)S(1)} all-reduce(f32[13312]{0:T(1024)S(1)} %add_dynamic-update-slice_fusion), channel_id=1, replica_groups=mesh['dp'=16,'tensor'=2] {'dp'}, use_global_device_ids=true, to_apply=%region_64.65 | all-reduce | flops 13312 | bytes 106496 | tf_op jit(solution)/shard_map/psum | solution.py:333
  1186.4 17.8 %all-gather.19.cloned.1.call-done = bf16[1024,512]{1,0:T(8,128)(2,1)} async-done(((bf16[64,512]{1,0:T(8,128)(2,1)}), bf16[1024,512]{1,0:T(8,128)(2,1)}) %all-gather.19.cloned.1.call-update) | async-done | bytes 1048592 | tf_op jit(solution)/shard_map/all_gather | solution.py:99
  1207.0 36.0 %all-gather.15.cloned.1.call-done = bf16[1024,512]{1,0:T(8,128)(2,1)} async-done(((bf16[64,512]{1,0:T(8,128)(2,1)}), bf16[1024,512]{1,0:T(8,128)(2,1)}) %all-gather.15.cloned.1.call-update) | async-done | bytes 1048592 | tf_op jit(solution)/shard_map/all_gather | solution.py:99
  1245.9 36.0 %all-gather.17.cloned.1.call-done = bf16[512,1024]{1,0:T(8,128)(2,1)} async-done(((bf16[32,1024]{1,0:T(8,128)(2,1)}), bf16[512,1024]{1,0:T(8,128)(2,1)}) %all-gather.17.cloned.1.call-update) | async-done | bytes 1048592 | tf_op jit(solution)/shard_map/all_gather | solution.py:99
  1284.7 36.1 %all-gather.11.cloned.1.call-done = bf16[1024,512]{1,0:T(8,128)(2,1)} async-done(((bf16[64,512]{1,0:T(8,128)(2,1)}), bf16[1024,512]{1,0:T(8,128)(2,1)}) %all-gather.11.cloned.1.call-update) | async-done | bytes 1048592 | tf_op jit(solution)/shard_map/all_gather | solution.py:99
  1323.6 36.0 %all-gather.13.cloned.1.call-done = bf16[1024,512]{1,0:T(8,128)(2,1)} async-done(((bf16[64,512]{1,0:T(8,128)(2,1)}), bf16[1024,512]{1,0:T(8,128)(2,1)}) %all-gather.13.cloned.1.call-update) | async-done | bytes 1048592 | tf_op jit(solution)/shard_map/all_gather | solution.py:99
  1362.5 48.7 %all-gather.29.cloned.1.call-done = bf16[2048,1024]{1,0:T(8,128)(2,1)} async-done(((bf16[128,1024]{1,0:T(8,128)(2,1)}), bf16[2048,1024]{1,0:T(8,128)(2,1)}) %all-gather.29.cloned.1.call-update) | async-done | bytes 4194320 | tf_op jit(solution)/shard_map/all_gather | solution.py:99
  1411.2 6.6 convert_element_type.662
  1417.9 44.3 %all-gather.27.cloned.1.call-done = bf16[1024,2048]{1,0:T(8,128)(2,1)} async-done(((bf16[64,2048]{1,0:T(8,128)(2,1)}), bf16[1024,2048]{1,0:T(8,128)(2,1)}) %all-gather.27.cloned.1.call-update) | async-done | bytes 4194320 | tf_op jit(solution)/shard_map/all_gather | solution.py:99
  1462.2 6.7 convert_element_type.660
  (591 shorter events, 278.9 us)
Async XLA Ops:
  7.2 59.5 %copy-start = (bf16[1024,512]{1,0:T(8,128)(2,1)S(1)}, bf16[1024,512]{1,0:T(8,128)(2,1)}, u32[]{:S(2)}) copy-start(bf16[1024,512]{1,0:T(8,128)(2,1)} %param.43) | copy-start | bytes 3145732
  7.2 561.3 %reduce-scatter.25.cloned.1.call-start = ((), (), s32[]{:S(2)}) async-start(), calls=%async_computation.24 | async-start | bytes 1114112 | tf_op jit(solution)/shard_map/reduce_scatter | solution.py:98
  36.5 14.8 %copy-start.155 = (bf16[8,64,448]{2,1,0:T(8,128)(2,1)}, bf16[8,64,448]{2,1,0:T(8,128)(2,1)S(1)}, u32[]{:S(2)}) copy-start(bf16[8,64,448]{2,1,0:T(8,128)(2,1)S(1)} %convolution_convert_fusion.22) | copy-start | bytes 1376260
  38.2 35.9 %collective-permute-start = (bf16[448,1024]{1,0:T(8,128)(2,1)}, bf16[448,1024]{1,0:T(8,128)(2,1)}, u32[]{:S(2)}, u32[]{:S(2)}) collective-permute-start(bf16[448,1024]{1,0:T(8,128)(2,1)} %convolution_convert_fusion.14), channel_id=1, source_target_pairs={{0,1},{1,0},{2,3},{3,2},{4,5},{5,4},{6,7},{7,6},{8,9},{9,8},{10,11... | collective-permute-start | bytes 2752520 | tf_op jit(solution)/shard_map/ppermute | solution.py:93
  106.2 24.1 %copy-start.11 = (f32[448,1024]{1,0:T(8,128)S(1)}, f32[448,1024]{1,0:T(8,128)}, u32[]{:S(2)}) copy-start(f32[448,1024]{1,0:T(8,128)} %copy-done.10) | copy-start | bytes 5505028
  108.3 21.9 %collective-permute-start.1 = (bf16[448,1024]{1,0:T(8,128)(2,1)S(1)}, bf16[448,1024]{1,0:T(8,128)(2,1)S(1)}, u32[]{:S(2)}, u32[]{:S(2)}) collective-permute-start(bf16[448,1024]{1,0:T(8,128)(2,1)S(1)} %convolution_convert_fusion.13), channel_id=1, source_target_pairs={{0,1},{1,0},{2,3},{3,2},{4,5},{5,4},{6,7},{7,6},{8,9},{9,8},{10,11... | collective-permute-start | bytes 2752520 | tf_op jit(solution)/shard_map/ppermute | solution.py:93
  143.6 23.5 %collective-permute-start.6 = (bf16[448,1024]{1,0:T(8,128)(2,1)}, bf16[448,1024]{1,0:T(8,128)(2,1)}, u32[]{:S(2)}, u32[]{:S(2)}) collective-permute-start(bf16[448,1024]{1,0:T(8,128)(2,1)} %convolution_convert_fusion.16), channel_id=1, source_target_pairs={{0,1},{1,0},{2,3},{3,2},{4,5},{5,4},{6,7},{7,6},{8,9},{9,8},{10,11... | collective-permute-start | bytes 2752520 | tf_op jit(solution)/shard_map/ppermute | solution.py:93
  146.9 37.6 %collective-permute-start.2 = (bf16[448,1024]{1,0:T(8,128)(2,1)}, bf16[448,1024]{1,0:T(8,128)(2,1)}, u32[]{:S(2)}, u32[]{:S(2)}) collective-permute-start(bf16[448,1024]{1,0:T(8,128)(2,1)} %convolution_convert_fusion.18), channel_id=1, source_target_pairs={{0,1},{1,0},{2,3},{3,2},{4,5},{5,4},{6,7},{7,6},{8,9},{9,8},{10,11... | collective-permute-start | bytes 2752520 | tf_op jit(solution)/shard_map/ppermute | solution.py:93
  152.1 32.5 %copy-start.14 = (f32[448,1024]{1,0:T(8,128)S(1)}, f32[448,1024]{1,0:T(8,128)}, u32[]{:S(2)}) copy-start(f32[448,1024]{1,0:T(8,128)} %copy-done.13) | copy-start | bytes 5505028
  152.1 32.5 %copy-start.37 = (bf16[2,448,1024]{2,1,0:T(8,128)(2,1)S(1)}, bf16[2,448,1024]{2,1,0:T(8,128)(2,1)}, u32[]{:S(2)}) copy-start(bf16[2,448,1024]{2,1,0:T(8,128)(2,1)} %param.29) | copy-start | bytes 5505028
  210.0 15.3 %copy-start.22 = (bf16[1500,512]{0,1:T(8,128)(2,1)S(1)}, bf16[1500,512]{0,1:T(8,128)(2,1)}, u32[]{:S(2)}) copy-start(bf16[1500,512]{0,1:T(8,128)(2,1)} %copy.103) | copy-start | bytes 4608004
  233.4 20.4 %collective-permute-start.7 = (bf16[448,1024]{1,0:T(8,128)(2,1)}, bf16[448,1024]{1,0:T(8,128)(2,1)}, u32[]{:S(2)}, u32[]{:S(2)}) collective-permute-start(bf16[448,1024]{1,0:T(8,128)(2,1)} %convolution_convert_fusion.10), channel_id=1, source_target_pairs={{0,1},{1,0},{2,3},{3,2},{4,5},{5,4},{6,7},{7,6},{8,9},{9,8},{10,11... | collective-permute-start | bytes 2752520 | tf_op jit(solution)/shard_map/ppermute | solution.py:93
  242.4 11.4 copy-start.12
  247.9 8.9 copy-start.28
  265.5 9.1 slice-start
  265.5 9.1 slice-start.2
  265.5 9.1 slice-start.1
  265.5 9.7 slice-start.3
  285.2 19.5 %collective-permute-start.3 = (bf16[448,1024]{1,0:T(8,128)(2,1)}, bf16[448,1024]{1,0:T(8,128)(2,1)}, u32[]{:S(2)}, u32[]{:S(2)}) collective-permute-start(bf16[448,1024]{1,0:T(8,128)(2,1)} %convolution_convert_fusion.12), channel_id=1, source_target_pairs={{0,1},{1,0},{2,3},{3,2},{4,5},{5,4},{6,7},{7,6},{8,9},{9,8},{10,11... | collective-permute-start | bytes 2752520 | tf_op jit(solution)/shard_map/ppermute | solution.py:93
  336.6 18.5 %copy-start.9 = (f32[448,1024]{1,0:T(8,128)S(1)}, f32[448,1024]{1,0:T(8,128)}, u32[]{:S(2)}) copy-start(f32[448,1024]{1,0:T(8,128)} %copy-done.8) | copy-start | bytes 5505028
  336.6 18.4 %collective-permute-start.4 = (bf16[448,1024]{1,0:T(8,128)(2,1)S(1)}, bf16[448,1024]{1,0:T(8,128)(2,1)S(1)}, u32[]{:S(2)}, u32[]{:S(2)}) collective-permute-start(bf16[448,1024]{1,0:T(8,128)(2,1)S(1)} %convolution_convert_fusion.11), channel_id=1, source_target_pairs={{0,1},{1,0},{2,3},{3,2},{4,5},{5,4},{6,7},{7,6},{8,9},{9,8},{10,11... | collective-permute-start | bytes 2752520 | tf_op jit(solution)/shard_map/ppermute | solution.py:93
  367.1 23.3 %collective-permute-start.9 = (bf16[448,1024]{1,0:T(8,128)(2,1)S(1)}, bf16[448,1024]{1,0:T(8,128)(2,1)S(1)}, u32[]{:S(2)}, u32[]{:S(2)}) collective-permute-start(bf16[448,1024]{1,0:T(8,128)(2,1)S(1)} %convolution_convert_fusion.15), channel_id=1, source_target_pairs={{0,1},{1,0},{2,3},{3,2},{4,5},{5,4},{6,7},{7,6},{8,9},{9,8},{10,11... | collective-permute-start | bytes 2752520 | tf_op jit(solution)/shard_map/ppermute | solution.py:93
  370.7 33.6 %collective-permute-start.5 = (bf16[448,1024]{1,0:T(8,128)(2,1)S(1)}, bf16[448,1024]{1,0:T(8,128)(2,1)S(1)}, u32[]{:S(2)}, u32[]{:S(2)}) collective-permute-start(bf16[448,1024]{1,0:T(8,128)(2,1)S(1)} %convolution_convert_fusion.17), channel_id=1, source_target_pairs={{0,1},{1,0},{2,3},{3,2},{4,5},{5,4},{6,7},{7,6},{8,9},{9,8},{10,11... | collective-permute-start | bytes 2752520 | tf_op jit(solution)/shard_map/ppermute | solution.py:93
  414.7 154.6 %reduce-scatter.23.cloned.1.call-start = ((), (), s32[]{:S(2)}) async-start(), calls=%async_computation.22 | async-start | bytes 1114112 | tf_op jit(solution)/shard_map/reduce_scatter | solution.py:98
  416.9 13.1 copy-start.30
  416.9 13.1 copy-start.62
  416.9 13.1 copy-start.64
  450.9 142.4 %reduce-scatter.21.cloned.1.call-start = ((), (), s32[]{:S(2)}) async-start(), calls=%async_computation.20 | async-start | bytes 1114112 | tf_op jit(solution)/shard_map/reduce_scatter | solution.py:98
  451.2 15.0 %copy-start.41 = (bf16[448,512]{0,1:T(8,128)(2,1)S(1)}, bf16[448,512]{0,1:T(8,128)(2,1)}, u32[]{:S(2)}) copy-start(bf16[448,512]{0,1:T(8,128)(2,1)} %copy.110) | copy-start | bytes 1376260
  479.4 174.1 %reduce-scatter.19.cloned.1.call-start = ((), (), s32[]{:S(2)}) async-start(), calls=%async_computation.18 | async-start | bytes 1114112 | tf_op jit(solution)/shard_map/reduce_scatter | solution.py:98
  489.3 17.1 %collective-permute-start.10 = (bf16[448,1024]{1,0:T(8,128)(2,1)}, bf16[448,1024]{1,0:T(8,128)(2,1)}, u32[]{:S(2)}, u32[]{:S(2)}) collective-permute-start(bf16[448,1024]{1,0:T(8,128)(2,1)} %convolution_convert_fusion.9), channel_id=1, source_target_pairs={{0,1},{1,0},{2,3},{3,2},{4,5},{5,4},{6,7},{7,6},{8,9},{9,8},{10,11... | collective-permute-start | bytes 2752520 | tf_op jit(solution)/shard_map/ppermute | solution.py:93
  499.5 214.1 %reduce-scatter.15.cloned.1.call-start = ((), (), s32[]{:S(2)}) async-start(), calls=%async_computation.14 | async-start | bytes 1114112 | tf_op jit(solution)/shard_map/reduce_scatter | solution.py:98
  499.9 8.9 copy-start.26
  522.9 251.0 %reduce-scatter.17.cloned.1.call-start = ((), (), s32[]{:S(2)}) async-start(), calls=%async_computation.16 | async-start | bytes 1114112 | tf_op jit(solution)/shard_map/reduce_scatter | solution.py:98
  526.1 13.2 copy-start.73
  528.4 306.4 %reduce-scatter.11.cloned.1.call-start = ((), (), s32[]{:S(2)}) async-start(), calls=%async_computation.10 | async-start | bytes 1114112 | tf_op jit(solution)/shard_map/reduce_scatter | solution.py:98
  542.6 353.0 %reduce-scatter.13.cloned.1.call-start = ((), (), s32[]{:S(2)}) async-start(), calls=%async_computation.12 | async-start | bytes 1114112 | tf_op jit(solution)/shard_map/reduce_scatter | solution.py:98
  550.5 421.5 %reduce-scatter.29.cloned.1.call-start = ((), (), s32[]{:S(2)}) async-start(), calls=%async_computation.28 | async-start | bytes 4456448 | tf_op jit(solution)/shard_map/reduce_scatter | solution.py:98
  558.8 489.3 %reduce-scatter.27.cloned.1.call-start = ((), (), s32[]{:S(2)}) async-start(), calls=%async_computation.26 | async-start | bytes 4456448 | tf_op jit(solution)/shard_map/reduce_scatter | solution.py:98
  568.4 403.8 %copy-start.18 = (bf16[8,64,1500]{2,1,0:T(8,128)(2,1)S(1)}, bf16[8,64,1500]{2,1,0:T(8,128)(2,1)}, u32[]{:S(2)}) copy-start(bf16[8,64,1500]{2,1,0:T(8,128)(2,1)} %fusion.32) | copy-start | bytes 4608004
  568.4 609.5 %all-gather.25.cloned.1.call-start = ((), (), s32[]{:S(2)}) async-start(), calls=%async_computation.25 | async-start | bytes 1114112 | tf_op jit(solution)/shard_map/all_gather | solution.py:99
  569.2 611.5 %all-gather.23.cloned.1.call-start = ((), (), s32[]{:S(2)}) async-start(), calls=%async_computation.23 | async-start | bytes 1114112 | tf_op jit(solution)/shard_map/all_gather | solution.py:99
  569.8 613.8 %all-gather.21.cloned.1.call-start = ((), (), s32[]{:S(2)}) async-start(), calls=%async_computation.21 | async-start | bytes 1114112 | tf_op jit(solution)/shard_map/all_gather | solution.py:99
  593.3 610.9 %all-gather.19.cloned.1.call-start = ((), (), s32[]{:S(2)}) async-start(), calls=%async_computation.19 | async-start | bytes 1114112 | tf_op jit(solution)/shard_map/all_gather | solution.py:99
  653.5 589.6 %all-gather.15.cloned.1.call-start = ((), (), s32[]{:S(2)}) async-start(), calls=%async_computation.15 | async-start | bytes 1114112 | tf_op jit(solution)/shard_map/all_gather | solution.py:99
  713.6 568.3 %all-gather.17.cloned.1.call-start = ((), (), s32[]{:S(2)}) async-start(), calls=%async_computation.17 | async-start | bytes 1114112 | tf_op jit(solution)/shard_map/all_gather | solution.py:99
  773.9 546.9 %all-gather.11.cloned.1.call-start = ((), (), s32[]{:S(2)}) async-start(), calls=%async_computation.11 | async-start | bytes 1114112 | tf_op jit(solution)/shard_map/all_gather | solution.py:99
  834.8 524.9 %all-gather.13.cloned.1.call-start = ((), (), s32[]{:S(2)}) async-start(), calls=%async_computation.13 | async-start | bytes 1114112 | tf_op jit(solution)/shard_map/all_gather | solution.py:99
  895.6 515.6 %all-gather.29.cloned.1.call-start = ((), (), s32[]{:S(2)}) async-start(), calls=%async_computation.29 | async-start | bytes 4456448 | tf_op jit(solution)/shard_map/all_gather | solution.py:99
  972.0 490.2 %all-gather.27.cloned.1.call-start = ((), (), s32[]{:S(2)}) async-start(), calls=%async_computation.27 | async-start | bytes 4456448 | tf_op jit(solution)/shard_map/all_gather | solution.py:99
  976.1 36.9 %collective-permute-start.12 = (bf16[1500,512]{1,0:T(8,128)(2,1)}, bf16[1500,512]{1,0:T(8,128)(2,1)}, u32[]{:S(2)}, u32[]{:S(2)}) collective-permute-start(bf16[1500,512]{1,0:T(8,128)(2,1)} %fusion.36), channel_id=1, source_target_pairs={{0,1},{1,0},{2,3},{3,2},{4,5},{5,4},{6,7},{7,6},{8,9},{9,8},{10,11... | collective-permute-start | bytes 4608008 | tf_op jit(solution)/shard_map/ppermute | solution.py:298
  981.7 31.3 %copy-start.32 = (bf16[8,64,1500]{2,1,0:T(8,128)(2,1)S(1)}, bf16[8,64,1500]{2,1,0:T(8,128)(2,1)}, u32[]{:S(2)}) copy-start(bf16[8,64,1500]{2,1,0:T(8,128)(2,1)} %get-tuple-element.188) | copy-start | bytes 4608004
  981.7 31.3 %copy-start.60 = (bf16[1024,512]{1,0:T(8,128)(2,1)S(1)}, bf16[1024,512]{1,0:T(8,128)(2,1)}, u32[]{:S(2)}) copy-start(bf16[1024,512]{1,0:T(8,128)(2,1)} %param.44) | copy-start | bytes 3145732
  983.4 33.7 %copy-start.20 = (bf16[8,64,1500]{2,1,0:T(8,128)(2,1)S(1)}, bf16[8,64,1500]{2,1,0:T(8,128)(2,1)}, u32[]{:S(2)}) copy-start(bf16[8,64,1500]{2,1,0:T(8,128)(2,1)} %copy-done.19) | copy-start | bytes 4608004
  983.5 124.0 %collective-permute-start.8 = (bf16[448,1024]{1,0:T(8,128)(2,1)}, bf16[448,1024]{1,0:T(8,128)(2,1)}, u32[]{:S(2)}, u32[]{:S(2)}) collective-permute-start(bf16[448,1024]{1,0:T(8,128)(2,1)} %add_convert_fusion.1), channel_id=1, source_target_pairs={{0,1},{1,0},{2,3},{3,2},{4,5},{5,4},{6,7},{7,6},{8,9},{9,8},{10,11... | collective-permute-start | bytes 2752520 | tf_op jit(solution)/shard_map/ppermute | solution.py:93
  1052.9 36.9 %collective-permute-start.13 = (bf16[1500,512]{1,0:T(8,128)(2,1)}, bf16[1500,512]{1,0:T(8,128)(2,1)}, u32[]{:S(2)}, u32[]{:S(2)}) collective-permute-start(bf16[1500,512]{1,0:T(8,128)(2,1)} %fusion.37), channel_id=1, source_target_pairs={{0,1},{1,0},{2,3},{3,2},{4,5},{5,4},{6,7},{7,6},{8,9},{9,8},{10,11... | collective-permute-start | bytes 4608008 | tf_op jit(solution)/shard_map/ppermute | solution.py:298
  1061.5 45.9 %collective-permute-start.11 = (bf16[448,1024]{1,0:T(8,128)(2,1)}, bf16[448,1024]{1,0:T(8,128)(2,1)}, u32[]{:S(2)}, u32[]{:S(2)}) collective-permute-start(bf16[448,1024]{1,0:T(8,128)(2,1)} %add_convert_fusion), channel_id=1, source_target_pairs={{0,1},{1,0},{2,3},{3,2},{4,5},{5,4},{6,7},{7,6},{8,9},{9,8},{10,11... | collective-permute-start | bytes 2752520 | tf_op jit(solution)/shard_map/ppermute | solution.py:93
  1062.1 27.7 %copy-start.34 = (bf16[8,64,1500]{2,1,0:T(8,128)(2,1)S(1)}, bf16[8,64,1500]{2,1,0:T(8,128)(2,1)}, u32[]{:S(2)}) copy-start(bf16[8,64,1500]{2,1,0:T(8,128)(2,1)} %copy-done.33) | copy-start | bytes 4608004
  1094.6 12.9 copy-start.7
  1094.6 12.9 copy-start.109
  1094.6 12.9 copy-start.111
  1094.6 12.9 copy-start.113
  1094.6 12.9 copy-start.115
  1094.6 12.9 copy-start.117
  (144 other events, 471.5 us)
Sparse Core Ops, SparseCore 0:
  414.8 57.9 reduce-scatter.24
  476.4 56.6 reduce-scatter.22
  536.7 56.5 reduce-scatter.20
  596.8 56.6 reduce-scatter.18
  656.9 56.6 reduce-scatter.14
  717.1 56.7 reduce-scatter.16
  778.1 56.6 reduce-scatter.10
  838.9 56.6 reduce-scatter.12
  900.0 71.8 reduce-scatter.28
  976.2 71.8 reduce-scatter.26
  1050.3 36.9 all-gather.24
  1089.3 36.8 all-gather.22
  1128.3 36.9 all-gather.20
  1167.3 36.8 all-gather.18
  1206.2 36.8 all-gather.14
  1245.1 36.8 all-gather.16
  1283.9 36.8 all-gather.10
  1322.8 36.8 all-gather.12
  1361.9 49.3 all-gather.28
  1413.2 48.8 all-gather.26
